TPU v7x, 128 devices: a whole 4x4x4 slice. The times are simulated.
128 devices in a mesh: depth: 8 (over y_hi, x), freq: 16 (over y_lo, z, core).
Axes of the slice: x: 4, y: 4 (y_hi: 2, y_lo: 2; y = y_hi * 2 + y_lo), z: 4, core: 2. Of those that a mesh axis runs over, the one named last changes fastest.
Arguments:
- source: bfloat16 [16, 2, 1024, 256], P('freq'), may hold values from -6 to 6
- propagator: bfloat16 [8, 16, 2, 1024, 1024], P('depth', 'freq'), may hold values from -0.125 to 0.125
- transmission: float32 [8, 16, 1024], P('depth', 'freq'), may hold values from 0.5 to 1.5
- upgoing: bfloat16 [8, 16, 2, 1024, 256], P('depth', 'freq'), may hold values from -6 to 6
Outputs:
- gradient: float32 [8, 1024, 2, 1024], P('depth', 'freq')
All inputs are finite; a program needn't handle non-finite values.
Results may differ from a plain program's by a relative error of at most 0.013.
Values may be sent and summed in bfloat16 or wider, within the bound.
A program may use at most 64 MiB of HBM per device.

v0:
```python
import jax
import jax.numpy as jnp
from jax import lax
from jax.sharding import PartitionSpec as P


def shifted(block, axis, distance):
    devices = range(lax.axis_size(axis))
    route = [(i - distance, i) for i in devices if i - distance in devices]
    return lax.ppermute(block, axis, route)


def advance(panel, weight, factor):
    shots = panel.shape[1] // 2
    real_part = jnp.dot(weight[0], panel, preferred_element_type=jnp.float32)
    imag_part = jnp.dot(weight[1], panel, preferred_element_type=jnp.float32)
    out_real = real_part[:, :shots] - imag_part[:, shots:]
    out_imag = real_part[:, shots:] + imag_part[:, :shots]
    joined = jnp.concatenate([out_real, out_imag], axis=1)
    return (joined * factor[:, None]).astype(jnp.bfloat16)


def shards(source, propagator, transmission, upgoing):
    weight = propagator[0, 0]
    factor = transmission[0, 0]
    upward = upgoing[0, 0]
    width = weight.shape[1]
    shots = source.shape[3]
    level = lax.axis_index("depth")
    levels = lax.axis_size("depth")
    freqs = lax.axis_size("freq")
    rows_own = width // freqs
    start_panel = jnp.concatenate([source[0, 0], source[0, 1]], axis=1)
    incoming = start_panel
    outgoing = advance(incoming, weight, factor)
    for tick in range(1, levels):
        arrived = shifted(outgoing, "depth", 1)
        incoming = jnp.where(level == 0, start_panel, arrived)
        outgoing = advance(incoming, weight, factor)
    up_pair = jnp.concatenate([upward[0], upward[1]], axis=1)
    dims = (((1,), (1,)), ((), ()))
    up_turn = jnp.concatenate([upward[1], -upward[0]], axis=1)
    real_part = lax.dot_general(up_pair, outgoing, dims, preferred_element_type=jnp.float32)
    imag_part = lax.dot_general(up_turn, outgoing, dims, preferred_element_type=jnp.float32)
    summed = lax.psum_scatter(
        jnp.stack([real_part, imag_part], axis=1), "freq", scatter_dimension=0, tiled=True
    )
    scale = (2.0 * shots * freqs) ** (-0.5)
    return (summed * scale).reshape(1, rows_own, 2, width)


def solution(mesh):
    return jax.shard_map(
        shards,
        mesh=mesh,
        in_specs=(
            P("freq", None, None, None),
            P("depth", "freq", None, None, None),
            P("depth", "freq", None),
            P("depth", "freq", None, None, None),
        ),
        out_specs=P("depth", "freq", None, None),
        check_vma=False,
    )
```

profile of v0, /device:TPU:31, one launch (start us, length us, event | category | flops | bytes accessed | tf_op | source)
XLA Modules:
  0.0 320.8 jit_solution(3369518401736191603)
XLA Ops:
  8.2 3.0 fusion.64
  11.3 1.3 fusion.40
  13.6 1.3 collective-permute-start
  14.9 24.6 %collective-permute-done = bf16[1024,512]{0,1:T(8,128)(2,1)S(1)} collective-permute-done((bf16[1024,512]{0,1:T(8,128)(2,1)S(1)}, bf16[1024,512]{0,1:T(8,128)(2,1)S(1)}, u32[]{:S(2)}, u32[]{:S(2)}) %collective-permute-start) | collective-permute-done | bytes 1048608 | tf_op jit(solution)/shard_map/ppermute | solution.py:10
  39.5 2.9 fusion.67
  42.4 1.3 fusion.43
  44.5 1.3 collective-permute-start.1
  45.8 23.8 %collective-permute-done.1 = bf16[1024,512]{0,1:T(8,128)(2,1)S(1)} collective-permute-done((bf16[1024,512]{0,1:T(8,128)(2,1)S(1)}, bf16[1024,512]{0,1:T(8,128)(2,1)S(1)}, u32[]{:S(2)}, u32[]{:S(2)}) %collective-permute-start.1) | collective-permute-done | bytes 1048608 | tf_op jit(solution)/shard_map/ppermute | solution.py:10
  69.6 1.3 fusion.70
  71.0 1.3 fusion.46
  73.1 1.5 collective-permute-start.2
  74.6 22.7 %collective-permute-done.2 = bf16[1024,512]{0,1:T(8,128)(2,1)S(1)} collective-permute-done((bf16[1024,512]{0,1:T(8,128)(2,1)S(1)}, bf16[1024,512]{0,1:T(8,128)(2,1)S(1)}, u32[]{:S(2)}, u32[]{:S(2)}) %collective-permute-start.2) | collective-permute-done | bytes 1048608 | tf_op jit(solution)/shard_map/ppermute | solution.py:10
  97.3 1.3 fusion.73
  98.7 1.3 fusion.49
  100.8 1.3 collective-permute-start.3
  102.1 24.1 %collective-permute-done.3 = bf16[1024,512]{0,1:T(8,128)(2,1)S(1)} collective-permute-done((bf16[1024,512]{0,1:T(8,128)(2,1)S(1)}, bf16[1024,512]{0,1:T(8,128)(2,1)S(1)}, u32[]{:S(2)}, u32[]{:S(2)}) %collective-permute-start.3) | collective-permute-done | bytes 1048608 | tf_op jit(solution)/shard_map/ppermute | solution.py:10
  126.2 1.3 fusion.76
  127.5 1.3 fusion.52
  129.7 1.3 collective-permute-start.4
  131.0 24.8 %collective-permute-done.4 = bf16[1024,512]{0,1:T(8,128)(2,1)S(1)} collective-permute-done((bf16[1024,512]{0,1:T(8,128)(2,1)S(1)}, bf16[1024,512]{0,1:T(8,128)(2,1)S(1)}, u32[]{:S(2)}, u32[]{:S(2)}) %collective-permute-start.4) | collective-permute-done | bytes 1048608 | tf_op jit(solution)/shard_map/ppermute | solution.py:10
  155.8 1.3 fusion.79
  157.1 1.3 fusion.55
  159.3 1.5 collective-permute-start.5
  160.8 23.7 %collective-permute-done.5 = bf16[1024,512]{0,1:T(8,128)(2,1)S(1)} collective-permute-done((bf16[1024,512]{0,1:T(8,128)(2,1)S(1)}, bf16[1024,512]{0,1:T(8,128)(2,1)S(1)}, u32[]{:S(2)}, u32[]{:S(2)}) %collective-permute-start.5) | collective-permute-done | bytes 1048608 | tf_op jit(solution)/shard_map/ppermute | solution.py:10
  184.6 1.3 fusion.82
  185.9 1.3 fusion.58
  188.1 1.4 collective-permute-start.6
  189.6 23.0 %collective-permute-done.6 = bf16[1024,512]{0,1:T(8,128)(2,1)S(1)} collective-permute-done((bf16[1024,512]{0,1:T(8,128)(2,1)S(1)}, bf16[1024,512]{0,1:T(8,128)(2,1)S(1)}, u32[]{:S(2)}, u32[]{:S(2)}) %collective-permute-start.6) | collective-permute-done | bytes 1048608 | tf_op jit(solution)/shard_map/ppermute | solution.py:10
  212.6 1.3 fusion.85
  213.9 1.3 fusion.61
  218.3 4.1 %pad_maximum_fusion = f32[1024,2,1024]{2,0,1:T(8,128)} fusion(f32[1024,1,1024]{2,0,1:T(8,128)S(1)} %convolution_bitcast_fusion, f32[1024,1,1024]{2,0,1:T(8,128)S(1)} %convolution_bitcast_fusion.1), kind=kLoop, calls=%fused_computation | loop fusion | flops 2097152 | bytes 16777216 | tf_op jit(solution)/shard_map/stack | solution.py:46
  222.4 89.2 %reduce-scatter.2.cloned.1.call-done = f32[64,2,1024]{2,0,1:T(8,128)} async-done(((f32[1024,2,1024]{2,0,1:T(8,128)}), f32[64,2,1024]{2,0,1:T(8,128)}) %reduce-scatter.2.cloned.1.call-update) | async-done | bytes 524304 | tf_op jit(solution)/shard_map/reduce_scatter | solution.py:45
  (34 shorter events, 13.0 us)
Async XLA Ops:
  6.5 305.1 %reduce-scatter.2.cloned.1.call-start = ((), (), s32[]{:S(2)}) async-start(), calls=%async_computation.1 | async-start | bytes 8912896 | tf_op jit(solution)/shard_map/reduce_scatter | solution.py:45
  8.2 3.0 copy-start.2
  12.6 0.7 copy-start.1
  13.6 25.9 %collective-permute-start = (bf16[1024,512]{0,1:T(8,128)(2,1)S(1)}, bf16[1024,512]{0,1:T(8,128)(2,1)S(1)}, u32[]{:S(2)}, u32[]{:S(2)}) collective-permute-start(bf16[1024,512]{0,1:T(8,128)(2,1)S(1)} %fusion), channel_id=1, source_target_pairs={{0,16},{16,32},{32,48},{48,64},{64,80},{80,96},{96,112},{1,17},{17... | collective-permute-start | bytes 3145736 | tf_op jit(solution)/shard_map/ppermute | solution.py:10
  14.9 27.5 %copy-start.3 = (bf16[1,1,2,1024,1024]{4,3,2,1,0:T(8,128)(2,1)S(1)}, bf16[1,1,2,1024,1024]{4,3,2,1,0:T(8,128)(2,1)}, u32[]{:S(2)}) copy-start(bf16[1,1,2,1024,1024]{4,3,2,1,0:T(8,128)(2,1)} %param.5) | copy-start | bytes 12582916
  44.5 25.1 %collective-permute-start.1 = (bf16[1024,512]{0,1:T(8,128)(2,1)S(1)}, bf16[1024,512]{0,1:T(8,128)(2,1)S(1)}, u32[]{:S(2)}, u32[]{:S(2)}) collective-permute-start(bf16[1024,512]{0,1:T(8,128)(2,1)S(1)} %fusion.1), channel_id=1, source_target_pairs={{0,16},{16,32},{32,48},{48,64},{64,80},{80,96},{96,112},{1,17},{17... | collective-permute-start | bytes 3145736 | tf_op jit(solution)/shard_map/ppermute | solution.py:10
  73.1 24.2 %collective-permute-start.2 = (bf16[1024,512]{0,1:T(8,128)(2,1)S(1)}, bf16[1024,512]{0,1:T(8,128)(2,1)S(1)}, u32[]{:S(2)}, u32[]{:S(2)}) collective-permute-start(bf16[1024,512]{0,1:T(8,128)(2,1)S(1)} %fusion.2), channel_id=1, source_target_pairs={{0,16},{16,32},{32,48},{48,64},{64,80},{80,96},{96,112},{1,17},{17... | collective-permute-start | bytes 3145736 | tf_op jit(solution)/shard_map/ppermute | solution.py:10
  100.8 25.4 %collective-permute-start.3 = (bf16[1024,512]{0,1:T(8,128)(2,1)S(1)}, bf16[1024,512]{0,1:T(8,128)(2,1)S(1)}, u32[]{:S(2)}, u32[]{:S(2)}) collective-permute-start(bf16[1024,512]{0,1:T(8,128)(2,1)S(1)} %fusion.3), channel_id=1, source_target_pairs={{0,16},{16,32},{32,48},{48,64},{64,80},{80,96},{96,112},{1,17},{17... | collective-permute-start | bytes 3145736 | tf_op jit(solution)/shard_map/ppermute | solution.py:10
  129.7 26.1 %collective-permute-start.4 = (bf16[1024,512]{0,1:T(8,128)(2,1)S(1)}, bf16[1024,512]{0,1:T(8,128)(2,1)S(1)}, u32[]{:S(2)}, u32[]{:S(2)}) collective-permute-start(bf16[1024,512]{0,1:T(8,128)(2,1)S(1)} %fusion.4), channel_id=1, source_target_pairs={{0,16},{16,32},{32,48},{48,64},{64,80},{80,96},{96,112},{1,17},{17... | collective-permute-start | bytes 3145736 | tf_op jit(solution)/shard_map/ppermute | solution.py:10
  159.3 25.3 %collective-permute-start.5 = (bf16[1024,512]{0,1:T(8,128)(2,1)S(1)}, bf16[1024,512]{0,1:T(8,128)(2,1)S(1)}, u32[]{:S(2)}, u32[]{:S(2)}) collective-permute-start(bf16[1024,512]{0,1:T(8,128)(2,1)S(1)} %fusion.5), channel_id=1, source_target_pairs={{0,16},{16,32},{32,48},{48,64},{64,80},{80,96},{96,112},{1,17},{17... | collective-permute-start | bytes 3145736 | tf_op jit(solution)/shard_map/ppermute | solution.py:10
  187.8 1.7 copy-start
  188.1 24.5 %collective-permute-start.6 = (bf16[1024,512]{0,1:T(8,128)(2,1)S(1)}, bf16[1024,512]{0,1:T(8,128)(2,1)S(1)}, u32[]{:S(2)}, u32[]{:S(2)}) collective-permute-start(bf16[1024,512]{0,1:T(8,128)(2,1)S(1)} %fusion.6), channel_id=1, source_target_pairs={{0,16},{16,32},{32,48},{48,64},{64,80},{80,96},{96,112},{1,17},{17... | collective-permute-start | bytes 3145736 | tf_op jit(solution)/shard_map/ppermute | solution.py:10
Sparse Core Ops, SparseCore 0:
  222.6 89.0 reduce-scatter.1
where the time goes:
time: 326 us; the launch traced here: 321 us
  waiting for transfers between devices  256 us (79%)
  matrix products  27 us (8%)
  between operations  13.8 us (4%)
  other arithmetic  11.4 us (3%)
  starting transfers between devices  9.58 us (3%)
    ppermute x7, waiting for transfers between devices, shifted(): return lax.ppermute(block, axis, route)  167 us
    reduce_scatter x1, waiting for transfers between devices, shards(): lax.psum_scatter(jnp.stack([real_part, imag_part], axis=1), 'freq', scatt...  89.2 us
    dot_general x8, matrix products, advance(): imag_part = jnp.dot(weight[1], panel, preferred_element_type=jnp.float32)  13.9 us
    dot_general x8, matrix products, advance(): real_part = jnp.dot(weight[0], panel, preferred_element_type=jnp.float32)  10.6 us
    ppermute x7, starting transfers between devices, shifted(): return lax.ppermute(block, axis, route)  9.58 us
  transfers between devices with their start and end apart: 8, of which 8 were waited for; matrix products, arithmetic and copies ran while one was open for 0% of the time, Pallas kernels for 0%

commit v1 on v0

v1 whole, which is shorter than its diff:
```python
import functools

import jax
import jax.numpy as jnp
from jax import lax
from jax.experimental import pallas as pl
from jax.experimental.pallas import tpu as pltpu
from jax.sharding import PartitionSpec as P

MESH = pl.DeviceIdType.MESH
BF16 = jnp.bfloat16
F32 = jnp.float32

CHUNKS = 8
TILE = 256
ORDERS = ((1, 2, 4), (2, 4, 1), (4, 1, 2))
TILE_ORDER = (0, 3, 6, 1, 4, 7, 2, 5)


def order_of(tile):
    return ORDERS[tile // 3]


def chip_at(z, y, relative):
    near = (z, z + 1 - 2 * (z % 2), 3 - z, (z + 2) % 4)[relative % 4]
    return (1 - y if relative >= 4 else y), near


def dot_nt(a, b):
    return lax.dot_general(a, b, (((1,), (1,)), ((), ())), preferred_element_type=F32)


def dot_nn(a, b):
    return lax.dot_general(a, b, (((1,), (0,)), ((), ())), preferred_element_type=F32)


def kernel(
    levels, scale,
    src_hbm, w_hbm, t_hbm, u_hbm, out_ref,
    src_ref, w_ref, t_ref, u_ref, lhs_ref, p_ref, q_ref, acc_ref, s_ref, r1_ref, r2_ref, r3_ref,
    load_sem, uload_sem, usend_sem, urecv_sem, psend_sem, precv_sem, qsend_sem, qrecv_sem, ssend_sem, srecv_sem,
):
    level = lax.axis_index("depth")
    freq = lax.axis_index("freq")
    core = freq % 2
    z = (freq // 2) % 4
    y = freq // 8
    partner = (level, freq + 1 - 2 * core)
    after = (level + 1, freq)
    before = (level - 1, freq)

    def freq_at(relative):
        y_at, z_at = chip_at(z, y, relative)
        return y_at * 8 + z_at * 2 + core

    def block_at(relative):
        y_at, z_at = chip_at(z, y, relative)
        return y_at * 4 + z_at

    shots = p_ref.shape[1]
    width = p_ref.shape[2]
    count = shots // CHUNKS
    half = shots // 2
    rows = out_ref.shape[1]
    tiles = width // TILE
    kept = u_ref.shape[2]

    src_copy = pltpu.make_async_copy(src_hbm, src_ref, load_sem.at[0])
    t_copy = pltpu.make_async_copy(t_hbm, t_ref, load_sem.at[1])
    w_copies = [
        pltpu.make_async_copy(
            w_hbm.at[:, pl.ds(m * TILE, TILE), :], w_ref.at[:, pl.ds(m * TILE, TILE), :], load_sem.at[2 + m]
        )
        for m in range(tiles)
    ]
    u_copies = [
        pltpu.make_async_copy(u_hbm.at[:, block_at(r), core], u_ref.at[0, :, r], uload_sem.at[r]) for r in range(kept)
    ]

    @pl.when(level == 0)
    def _():
        src_copy.start()

    t_copy.start()
    for copy in w_copies:
        copy.start()
    for copy in u_copies:
        copy.start()

    barrier = pltpu.get_barrier_semaphore()
    sides = [partner] + [(level, freq_at(bit)) for bit in (1, 2, 4)]
    for device in sides:
        pl.semaphore_signal(barrier, inc=1, device_id=device, device_id_type=MESH)

    @pl.when(level > 0)
    def _():
        pl.semaphore_signal(barrier, inc=1, device_id=before, device_id_type=MESH)

    @pl.when(level < levels - 1)
    def _():
        pl.semaphore_signal(barrier, inc=1, device_id=after, device_id_type=MESH)

    inner = (level > 0) & (level < levels - 1)

    @pl.when(inner)
    def _():
        pl.semaphore_wait(barrier, len(sides) + 2)

    @pl.when(jnp.logical_not(inner))
    def _():
        pl.semaphore_wait(barrier, len(sides) + 1)

    def u_swap(r):
        return pltpu.make_async_remote_copy(
            u_hbm.at[:, block_at(r), 1 - core], u_ref.at[1, :, r], usend_sem.at[r], urecv_sem.at[r],
            device_id=partner, device_id_type=MESH,
        )

    for r in range(kept):
        u_swap(r).start()

    def make_lhs():
        for copy in u_copies:
            copy.wait()
        for r in range(kept):
            u_swap(r).wait_recv()
        for part in range(2):
            span = pl.ds(part * half, half)
            for slot in range(2):
                real = u_ref[slot, 0, :, :, span].reshape(kept * rows, half)
                imag = u_ref[slot, 1, :, :, span].reshape(kept * rows, half)
                lhs_ref[part, 0, :, pl.ds(slot * 2 * half, half)] = real
                lhs_ref[part, 0, :, pl.ds(slot * 2 * half + half, half)] = imag
                lhs_ref[part, 1, :, pl.ds(slot * 2 * half, half)] = imag
                lhs_ref[part, 1, :, pl.ds(slot * 2 * half + half, half)] = -real

    @pl.when(level == 0)
    def _():
        src_copy.wait()
        for plane in range(2):
            for part in range(2):
                p_ref[plane, pl.ds(part * half, half), :] = src_ref[plane, :, pl.ds(part * half, half)].T

    @pl.when(level > 0)
    def _():
        make_lhs()

    t_copy.wait()
    for copy in w_copies:
        copy.wait()

    def span_of(c):
        return pl.ds(pl.multiple_of(c * count, count), count)

    def onward(c):
        return pltpu.make_async_remote_copy(
            q_ref.at[0, :, span_of(c), :], p_ref.at[:, span_of(c), :], psend_sem.at[c], precv_sem.at[c],
            device_id=after, device_id_type=MESH,
        )

    def across(c):
        return pltpu.make_async_remote_copy(
            q_ref.at[0, :, span_of(c), :], q_ref.at[1, :, span_of(c), :], qsend_sem.at[c], qrecv_sem.at[c],
            device_id=partner, device_id_type=MESH,
        )

    def advance(c):
        span = span_of(c)

        @pl.when(level > 0)
        def _():
            onward(c).wait_recv()

        real = p_ref[0, span, :]
        imag = p_ref[1, span, :]
        plain = jnp.concatenate([real, imag], axis=0)
        turned = jnp.concatenate([-imag, real], axis=0)
        for m in range(tiles):
            cols = pl.ds(m * TILE, TILE)
            total = dot_nt(plain, w_ref[0, cols, :]) + dot_nt(turned, w_ref[1, cols, :])
            total = (total * t_ref[:, cols]).astype(BF16)
            q_ref[0, 0, span, cols] = total[:count]
            q_ref[0, 1, span, cols] = total[count:]

        @pl.when(level < levels - 1)
        def _():
            onward(c).start()

        across(c).start()

    def product(part, plane, cols):
        span = pl.ds(part * half, half)
        rhs = jnp.concatenate([q_ref[slot, p, span, cols] for slot in range(2) for p in range(2)], axis=0)
        return dot_nn(lhs_ref[part, plane], rhs)

    def first(c, carry):
        advance(c)
        return carry

    lax.fori_loop(0, CHUNKS // 2, first, 0)

    @pl.when(level == 0)
    def _():
        make_lhs()

    for c in range(CHUNKS // 2):
        across(c).wait_recv()

    def second(c, carry):
        advance(CHUNKS // 2 + c)
        for plane in range(2):
            cols = pl.ds(pl.multiple_of(c * TILE, TILE), TILE)
            acc_ref[plane, c] = product(0, plane, cols)
        return carry

    lax.fori_loop(0, tiles, second, 0)
    for c in range(CHUNKS // 2, CHUNKS):
        across(c).wait_recv()

    landing = (r1_ref, r2_ref, r3_ref)

    def piece(tile, step, r):
        bit = order_of(tile)[step]
        at = sum(4 >> s for s in range(step))
        index = at + sum((1 << i) for i, b in enumerate(order_of(tile)[step + 1:]) if r & b)
        cols = pl.ds(tile * TILE, TILE)
        return pltpu.make_async_remote_copy(
            s_ref.at[r, :, cols], landing[step].at[r - bit, :, cols],
            ssend_sem.at[tile, index], srecv_sem.at[tile, index],
            device_id=(level, freq_at(bit)), device_id_type=MESH,
        )

    def sets(tile):
        a, b, c = order_of(tile)
        return ((a + b + c, a + b, a + c, a), (b + c, b), (c,))

    def kept_block(tile, r):
        return acc_ref[tile // tiles, tile % tiles, pl.ds(r * rows, rows), :]

    for tile in TILE_ORDER:
        plane, col = tile // tiles, tile % tiles
        cols = pl.ds(tile * TILE, TILE)
        acc_ref[plane, col] += product(1, plane, pl.ds(col * TILE, TILE))
        for r in sets(tile)[0]:
            s_ref[r, :, cols] = kept_block(tile, r).astype(BF16)
            piece(tile, 0, r).start()

    for tile in TILE_ORDER:
        a, b, c = order_of(tile)
        cols = pl.ds(tile * TILE, TILE)
        for r in (b + c, b):
            piece(tile, 0, r + a).wait_recv()
            s_ref[r, :, cols] = (kept_block(tile, r) + r1_ref[r, :, cols].astype(F32)).astype(BF16)
            piece(tile, 1, r).start()

    for tile in TILE_ORDER:
        a, b, c = order_of(tile)
        cols = pl.ds(tile * TILE, TILE)
        piece(tile, 0, c + a).wait_recv()
        piece(tile, 1, c + b).wait_recv()
        s_ref[c, :, cols] = (
            kept_block(tile, c) + r1_ref[c, :, cols].astype(F32) + r2_ref[c, :, cols].astype(F32)
        ).astype(BF16)
        piece(tile, 2, c).start()

    for tile in TILE_ORDER:
        a, b, c = order_of(tile)
        cols = pl.ds(tile * TILE, TILE)
        piece(tile, 0, a).wait_recv()
        piece(tile, 1, b).wait_recv()
        piece(tile, 2, c).wait_recv()
        total = kept_block(tile, 0) + r1_ref[0, :, cols].astype(F32)
        total = total + r2_ref[0, :, cols].astype(F32) + r3_ref[0, :, cols].astype(F32)
        out_ref[tile // tiles, :, pl.ds((tile % tiles) * TILE, TILE)] = total * scale

    for r in range(kept):
        u_swap(r).wait_send()
    for c in range(CHUNKS):
        across(c).wait_send()

        @pl.when(level < levels - 1)
        def _():
            onward(c).wait_send()

    for tile in TILE_ORDER:
        for step, leaving in enumerate(sets(tile)):
            for r in leaving:
                piece(tile, step, r).wait_send()


def shards(source, propagator, transmission, upgoing):
    levels = lax.axis_size("depth")
    freqs = lax.axis_size("freq")
    width = propagator.shape[3]
    shots = source.shape[3]
    rows = width // freqs
    kept = freqs // 2
    tiles = width // TILE
    scale = (2.0 * shots * freqs) ** (-0.5)
    dma = pltpu.SemaphoreType.DMA
    summed = pl.pallas_call(
        functools.partial(kernel, levels, scale),
        out_shape=jax.ShapeDtypeStruct((2, rows, width), F32),
        in_specs=[pl.BlockSpec(memory_space=pl.ANY)] * 4,
        out_specs=pl.BlockSpec(memory_space=pltpu.VMEM),
        scratch_shapes=[
            pltpu.VMEM((2, width, shots), BF16),
            pltpu.VMEM((2, width, width), BF16),
            pltpu.VMEM((1, width), F32),
            pltpu.VMEM((2, 2, kept, rows, shots), BF16),
            pltpu.VMEM((2, 2, kept * rows, 2 * shots), BF16),
            pltpu.VMEM((2, shots, width), BF16),
            pltpu.VMEM((2, 2, shots, width), BF16),
            pltpu.VMEM((2, tiles, kept * rows, TILE), F32),
            pltpu.VMEM((kept, rows, 2 * width), BF16),
            pltpu.VMEM((kept, rows, 2 * width), BF16),
            pltpu.VMEM((kept, rows, 2 * width), BF16),
            pltpu.VMEM((kept, rows, 2 * width), BF16),
            dma((2 + tiles,)),
            dma((kept,)),
            dma((kept,)),
            dma((kept,)),
            dma((CHUNKS,)),
            dma((CHUNKS,)),
            dma((CHUNKS,)),
            dma((CHUNKS,)),
            dma((2 * tiles, 7)),
            dma((2 * tiles, 7)),
        ],
        compiler_params=pltpu.CompilerParams(
            collective_id=0, has_side_effects=True, vmem_limit_bytes=60 * 1024 * 1024
        ),
    )(
        source.reshape(2, width, shots),
        propagator.reshape(2, width, width),
        transmission.reshape(1, width),
        upgoing.reshape(2, kept, 2, rows, shots),
    )
    return jnp.transpose(summed, (1, 0, 2)).reshape(1, rows, 2, width)


def solution(mesh):
    return jax.shard_map(
        shards,
        mesh=mesh,
        in_specs=(
            P("freq", None, None, None),
            P("depth", "freq", None, None, None),
            P("depth", "freq", None),
            P("depth", "freq", None, None, None),
        ),
        out_specs=P("depth", "freq", None, None),
        check_vma=False,
    )
```

time: 326 us -> 93.8 us (0.29); the launches traced: 321 us -> 92.6 us
  waiting for transfers between devices: 256 us -> 0 us
  Pallas kernels: 0 us -> 90.3 us
  matrix products: 27 us -> 0 us
  between operations: 13.8 us -> 0.01 us
  other arithmetic: 11.4 us -> 0 us
  starting transfers between devices: 9.58 us -> 0 us
    ppermute x7 -> x0, waiting for transfers between devices: 167 us -> none  [shifted(): return lax.ppermute(block, axis, route)]
    pallas_call x0 -> x1, Pallas kernels: none -> 90.3 us  [shards(): pl.pallas_call(functools.partial(kernel, levels, scale), out_shape=jax.Sh...]
    reduce_scatter x1 -> x0, waiting for transfers between devices: 89.2 us -> none  [shards(): lax.psum_scatter(jnp.stack([real_part, imag_part], axis=1), 'freq', scatt...]
    dot_general x18 -> x0, matrix products: 27 us -> none  [the longest x8 13.9 us: advance(): imag_part = jnp.dot(weight[1], panel, preferred_element_type=jnp.float32)]
    ppermute x7 -> x0, starting transfers between devices: 9.58 us -> none  [shifted(): return lax.ppermute(block, axis, route)]
    sub x8 -> x0, other arithmetic: 4.41 us -> none  [advance(): out_real = real_part[:, :shots] - imag_part[:, shots:]]
    another operation x1 -> x0, other arithmetic: 4.09 us -> none  [shards(): jnp.stack([real_part, imag_part], axis=1)]
  transfers between devices with their start and end apart: 8 -> 0, of which waited for: 8 -> 0; matrix products, arithmetic and copies ran while one was open for 0% -> 0% of each run, Pallas kernels for 0% -> 0%
where the time goes in v1:
time: 93.8 us; the launch traced here: 92.6 us
  Pallas kernels  90.3 us (96%)
  local copies, waits for them, and re-layouts  2.24 us (2%)
    pallas_call x1, Pallas kernels, shards(): pl.pallas_call(functools.partial(kernel, levels, scale), out_shape=jax.Sh...  90.3 us
    reshape x1, local copies, waits for them, and re-layouts, shards(): return jnp.transpose(summed, (1, 0, 2)).reshape(1, rows, 2, width)  2.24 us

profile of v1, /device:TPU:31, one launch (start us, length us, event | category | flops | bytes accessed | tf_op | source)
XLA Modules:
  0.0 92.6 jit_solution(3911957967373725145)
XLA Ops:
  0.0 90.3 %shard_map.46 = f32[2,64,1024]{2,1,0:T(8,128)} custom-call(bf16[2,1024,256]{2,1,0:T(8,128)(2,1)} %bitcast.9, bf16[2,1024,1024]{2,1,0:T(8,128)(2,1)} %bitcast.7, f32[1,1024]{1,0:T(1,128)} %bitcast.11, bf16[2,8,2,64,256]{4,3,2,1,0:T(8,128)(2,1)} %bitcast.10), custom_call_target="tpu_custom_call" | custom-call | tf_op jit(solution)/shard_map/pallas_call | solution.py:301
  90.3 2.2 %copy.5 = f32[1,64,2,1024]{3,2,1,0:T(2,128)} copy(f32[1,64,2,1024]{3,1,2,0:T(8,128)} %bitcast.8) | data formatting | bytes 1048576 | tf_op jit(solution)/shard_map/reshape | solution.py:339

commit v2 on v1

v2 whole, which is shorter than its diff:
```python
import functools

import jax
import jax.numpy as jnp
from jax import lax
from jax.experimental import pallas as pl
from jax.experimental.pallas import tpu as pltpu
from jax.sharding import PartitionSpec as P

MESH = pl.DeviceIdType.MESH
BF16 = jnp.bfloat16
F32 = jnp.float32

CHUNKS = 16
PIECES = 2
TILE = 256
ORDERS = ((1, 2, 4), (2, 4, 1), (4, 1, 2))
TILE_ORDER = (0, 3, 6, 1, 4, 7, 2, 5)


def order_of(tile):
    return ORDERS[tile // 3]


def chip_at(z, y, relative):
    near = (z, z + 1 - 2 * (z % 2), 3 - z, (z + 2) % 4)[relative % 4]
    return (1 - y if relative >= 4 else y), near


def dot_nt(a, b):
    return lax.dot_general(a, b, (((1,), (1,)), ((), ())), preferred_element_type=F32)


def dot_nn(a, b):
    return lax.dot_general(a, b, (((1,), (0,)), ((), ())), preferred_element_type=F32)


def kernel(
    levels, scale,
    src_hbm, w_hbm, t_hbm, u_hbm, out_ref,
    src_ref, w_ref, wt_ref, t_ref, u_ref, p_ref, q_ref, acc_ref, s_ref, r1_ref, r2_ref, r3_ref,
    load_sem, uload_sem, usend_sem, urecv_sem, psend_sem, precv_sem, qsend_sem, qrecv_sem, ssend_sem, srecv_sem,
):
    level = lax.axis_index("depth")
    freq = lax.axis_index("freq")
    core = freq % 2
    z = (freq // 2) % 4
    y = freq // 8
    partner = (level, freq + 1 - 2 * core)
    after = (level + 1, freq)
    before = (level - 1, freq)

    def freq_at(relative):
        y_at, z_at = chip_at(z, y, relative)
        return y_at * 8 + z_at * 2 + core

    def block_at(relative):
        y_at, z_at = chip_at(z, y, relative)
        return y_at * 4 + z_at

    count = p_ref.shape[2] // 2
    deep = p_ref.shape[3]
    width = deep * PIECES
    shots = count * CHUNKS
    half = shots // 2
    halfway = CHUNKS // 2
    kept = u_ref.shape[2]
    rows = u_ref.shape[3]
    tiles = width // TILE

    src_copy = pltpu.make_async_copy(src_hbm, src_ref, load_sem.at[0])
    t_copy = pltpu.make_async_copy(t_hbm, t_ref, load_sem.at[1])
    w_copies = [
        pltpu.make_async_copy(
            w_hbm.at[:, pl.ds(m * TILE, TILE), :], w_ref.at[:, pl.ds(m * TILE, TILE), :], load_sem.at[2 + m]
        )
        for m in range(tiles)
    ]
    u_copies = [
        pltpu.make_async_copy(u_hbm.at[:, block_at(r), core], u_ref.at[0, :, r], uload_sem.at[r]) for r in range(kept)
    ]

    @pl.when(level == 0)
    def _():
        src_copy.start()

    for copy in w_copies:
        copy.start()
    t_copy.start()
    for copy in u_copies:
        copy.start()

    barrier = pltpu.get_barrier_semaphore()
    sides = [partner] + [(level, freq_at(bit)) for bit in (1, 2, 4)]
    for device in sides:
        pl.semaphore_signal(barrier, inc=1, device_id=device, device_id_type=MESH)

    @pl.when(level > 0)
    def _():
        pl.semaphore_signal(barrier, inc=1, device_id=before, device_id_type=MESH)

    @pl.when(level < levels - 1)
    def _():
        pl.semaphore_signal(barrier, inc=1, device_id=after, device_id_type=MESH)

    def turn_source(part):
        for k in range(PIECES):
            for plane in range(2):
                block = src_ref[plane, pl.ds(k * deep, deep), pl.ds(part * half, half)].T
                p_ref[pl.ds(part * halfway, halfway), k, pl.ds(plane * count, count), :] = block.reshape(
                    halfway, count, deep
                )

    @pl.when(level == 0)
    def _():
        src_copy.wait()
        turn_source(0)

    inner = (level > 0) & (level < levels - 1)

    @pl.when(inner)
    def _():
        pl.semaphore_wait(barrier, len(sides) + 2)

    @pl.when(jnp.logical_not(inner))
    def _():
        pl.semaphore_wait(barrier, len(sides) + 1)

    def u_swap(r):
        return pltpu.make_async_remote_copy(
            u_hbm.at[:, block_at(r), 1 - core], u_ref.at[1, :, r], usend_sem.at[r], urecv_sem.at[r],
            device_id=partner, device_id_type=MESH,
        )

    for r in range(kept):
        u_swap(r).start()

    t_copy.wait()
    for m in range(tiles):
        w_copies[m].wait()

        @pl.when(level > 0)
        def _():
            for k in range(PIECES):
                for plane in range(2):
                    block = w_ref[plane, pl.ds(m * TILE, TILE), pl.ds(k * deep, deep)]
                    wt_ref[k, pl.ds(plane * deep, deep), pl.ds(m * TILE, TILE)] = block.T

    def onward(c, k):
        return pltpu.make_async_remote_copy(
            q_ref.at[0, c, k], p_ref.at[c, k], psend_sem.at[c, k], precv_sem.at[c, k],
            device_id=after, device_id_type=MESH,
        )

    def across(c):
        return pltpu.make_async_remote_copy(
            q_ref.at[0, c], q_ref.at[1, c], qsend_sem.at[c], qrecv_sem.at[c],
            device_id=partner, device_id_type=MESH,
        )

    def chunk_lhs(c, k):
        real = p_ref[c, k, pl.ds(0, count), :]
        imag = p_ref[c, k, pl.ds(count, count), :]
        return jnp.concatenate([real, imag], axis=0), jnp.concatenate([-imag, real], axis=0)

    def scaled(total, m):
        return (total * t_ref[:, pl.ds(m * deep, deep)]).astype(BF16)

    def open_chunks(b):
        sides = [[chunk_lhs(2 * b + i, k) for k in range(PIECES)] for i in range(2)]
        plain, turned = (
            jnp.concatenate(
                [jnp.concatenate([sides[i][k][which] for i in range(2)], axis=0) for k in range(PIECES)], axis=1
            )
            for which in range(2)
        )
        for m in range(PIECES):
            cols = pl.ds(m * deep, deep)
            total = scaled(dot_nt(plain, w_ref[0, cols, :]) + dot_nt(turned, w_ref[1, cols, :]), m)
            for i in range(2):
                q_ref[0, 2 * b + i, m] = total[i * 2 * count:(i + 1) * 2 * count]
                onward(2 * b + i, m).start()
        for i in range(2):
            across(2 * b + i).start()

    def advance(c):
        totals = [None] * PIECES
        for k in range(PIECES):
            onward(c, k).wait_recv()
            lhs = jnp.concatenate(chunk_lhs(c, k), axis=1)
            for m in range(PIECES):
                part = dot_nn(lhs, wt_ref[k, :, pl.ds(m * deep, deep)])
                totals[m] = part if k == 0 else totals[m] + part
                if k == PIECES - 1:
                    q_ref[0, c, m] = scaled(totals[m], m)

                    @pl.when(level < levels - 1)
                    def _():
                        onward(c, m).start()

        across(c).start()

    def product(part, plane, col):
        first = part * halfway
        k, cols = col * TILE // deep, pl.ds(pl.multiple_of(col * TILE % deep, TILE), TILE)
        lhs, rhs = [], []
        for slot in range(2):
            real = q_ref[slot, pl.ds(first, halfway), k, pl.ds(0, count), cols].reshape(half, TILE)
            imag = q_ref[slot, pl.ds(first, halfway), k, pl.ds(count, count), cols].reshape(half, TILE)
            u_real, u_imag = (
                u_ref[slot, p, :, :, pl.ds(part * half, half)].reshape(kept * rows, half) for p in range(2)
            )
            lhs += [u_imag, u_real] if plane else [u_real, u_imag]
            rhs += [real, -imag] if plane else [real, imag]
        return dot_nn(jnp.concatenate(lhs, axis=1), jnp.concatenate(rhs, axis=0))

    def first_half(tile):
        acc_ref[tile] = product(0, tile // tiles, tile % tiles)

    def ready(part):
        for c in range(part * halfway, (part + 1) * halfway):
            across(c).wait_recv()

    def swapped():
        for r in range(kept):
            u_copies[r].wait()
            u_swap(r).wait_recv()

    @pl.when(level == 0)
    def _():
        def opening(b, carry):
            open_chunks(b)
            return carry

        lax.fori_loop(0, halfway // 2, opening, 0)
        turn_source(1)
        lax.fori_loop(halfway // 2, halfway, opening, 0)
        swapped()
        ready(0)
        for tile in range(2 * tiles):
            first_half(tile)

    @pl.when(level > 0)
    def _():
        def early(c, carry):
            advance(c)
            return carry

        lax.fori_loop(0, halfway, early, 0)
        swapped()
        ready(0)
        for plane in range(2):
            def late(col, carry):
                advance(halfway + plane * tiles + col)
                acc_ref[plane * tiles + col] = product(0, plane, col)
                return carry

            lax.fori_loop(0, tiles, late, 0)

    ready(1)

    landing = (r1_ref, r2_ref, r3_ref)

    def piece(tile, step, r):
        bit = order_of(tile)[step]
        at = sum(4 >> s for s in range(step))
        index = at + sum((1 << i) for i, b in enumerate(order_of(tile)[step + 1:]) if r & b)
        return pltpu.make_async_remote_copy(
            s_ref.at[tile, r], landing[step].at[tile, r - bit],
            ssend_sem.at[tile, index], srecv_sem.at[tile, index],
            device_id=(level, freq_at(bit)), device_id_type=MESH,
        )

    def own(tile, r):
        return acc_ref[tile, pl.ds(r * rows, rows), :]

    for tile in TILE_ORDER:
        a, b, c = order_of(tile)
        acc_ref[tile] += product(1, tile // tiles, tile % tiles)
        for r in (a + b + c, a + b, a + c):
            s_ref[tile, r] = own(tile, r).astype(BF16)
            piece(tile, 0, r).start()

    for more in (True, False):
        for tile in TILE_ORDER:
            a, b, c = order_of(tile)
            r = b + c if more else b
            piece(tile, 0, r + a).wait_recv()
            s_ref[tile, r] = (own(tile, r) + r1_ref[tile, r].astype(F32)).astype(BF16)
            piece(tile, 1, r).start()

    for tile in TILE_ORDER:
        a, b, c = order_of(tile)
        piece(tile, 0, c + a).wait_recv()
        piece(tile, 1, c + b).wait_recv()
        s_ref[tile, c] = (own(tile, c) + r1_ref[tile, c].astype(F32) + r2_ref[tile, c].astype(F32)).astype(BF16)
        piece(tile, 2, c).start()

    for tile in TILE_ORDER:
        a, b, c = order_of(tile)
        s_ref[tile, a] = own(tile, a).astype(BF16)
        piece(tile, 0, a).start()

    for tile in TILE_ORDER:
        a, b, c = order_of(tile)
        piece(tile, 1, b).wait_recv()
        piece(tile, 2, c).wait_recv()
        piece(tile, 0, a).wait_recv()
        total = own(tile, 0) + r1_ref[tile, 0].astype(F32)
        total = total + r2_ref[tile, 0].astype(F32) + r3_ref[tile, 0].astype(F32)
        out_ref[tile // tiles, :, pl.ds((tile % tiles) * TILE, TILE)] = total * scale

    for r in range(kept):
        u_swap(r).wait_send()
    for c in range(CHUNKS):
        across(c).wait_send()

    @pl.when(level < levels - 1)
    def _():
        for c in range(CHUNKS):
            for k in range(PIECES):
                onward(c, k).wait_send()

    for tile in TILE_ORDER:
        a, b, c = order_of(tile)
        for r in (a + b + c, a + b, a + c, a):
            piece(tile, 0, r).wait_send()
        for r in (b + c, b):
            piece(tile, 1, r).wait_send()
        piece(tile, 2, c).wait_send()


def shards(source, propagator, transmission, upgoing):
    levels = lax.axis_size("depth")
    freqs = lax.axis_size("freq")
    width = propagator.shape[3]
    shots = source.shape[3]
    rows = width // freqs
    kept = freqs // 2
    tiles = width // TILE
    count = shots // CHUNKS
    deep = width // PIECES
    scale = (2.0 * shots * freqs) ** (-0.5)
    dma = pltpu.SemaphoreType.DMA
    summed = pl.pallas_call(
        functools.partial(kernel, levels, scale),
        out_shape=jax.ShapeDtypeStruct((2, rows, width), F32),
        in_specs=[pl.BlockSpec(memory_space=pl.ANY)] * 4,
        out_specs=pl.BlockSpec(memory_space=pltpu.VMEM),
        scratch_shapes=[
            pltpu.VMEM((2, width, shots), BF16),
            pltpu.VMEM((2, width, width), BF16),
            pltpu.VMEM((PIECES, 2 * deep, width), BF16),
            pltpu.VMEM((1, width), F32),
            pltpu.VMEM((2, 2, kept, rows, shots), BF16),
            pltpu.VMEM((CHUNKS, PIECES, 2 * count, deep), BF16),
            pltpu.VMEM((2, CHUNKS, PIECES, 2 * count, deep), BF16),
            pltpu.VMEM((2 * tiles, kept * rows, TILE), F32),
            pltpu.VMEM((2 * tiles, kept, rows, TILE), BF16),
            pltpu.VMEM((2 * tiles, kept, rows, TILE), BF16),
            pltpu.VMEM((2 * tiles, kept, rows, TILE), BF16),
            pltpu.VMEM((2 * tiles, kept, rows, TILE), BF16),
            dma((2 + tiles,)),
            dma((kept,)),
            dma((kept,)),
            dma((kept,)),
            dma((CHUNKS, PIECES)),
            dma((CHUNKS, PIECES)),
            dma((CHUNKS,)),
            dma((CHUNKS,)),
            dma((2 * tiles, 7)),
            dma((2 * tiles, 7)),
        ],
        compiler_params=pltpu.CompilerParams(
            collective_id=0, has_side_effects=True, vmem_limit_bytes=60 * 1024 * 1024
        ),
    )(
        source.reshape(2, width, shots),
        propagator.reshape(2, width, width),
        transmission.reshape(1, width),
        upgoing.reshape(2, kept, 2, rows, shots),
    )
    return jnp.transpose(summed, (1, 0, 2)).reshape(1, rows, 2, width)


def solution(mesh):
    return jax.shard_map(
        shards,
        mesh=mesh,
        in_specs=(
            P("freq", None, None, None),
            P("depth", "freq", None, None, None),
            P("depth", "freq", None),
            P("depth", "freq", None, None, None),
        ),
        out_specs=P("depth", "freq", None, None),
        check_vma=False,
    )
```

time: 93.8 us -> 82.1 us (0.88); the launches traced: 92.6 us -> 82 us
  Pallas kernels: 90.3 us -> 79.7 us
    pallas_call x1, Pallas kernels: 90.3 us -> 79.7 us  [shards(): pl.pallas_call(functools.partial(kernel, levels, scale), out_shape=jax.Sh...]
where the time goes in v2:
time: 82.1 us; the launch traced here: 82 us
  Pallas kernels  79.7 us (97%)
  local copies, waits for them, and re-layouts  2.24 us (3%)
    pallas_call x1, Pallas kernels, shards(): pl.pallas_call(functools.partial(kernel, levels, scale), out_shape=jax.Sh...  79.7 us
    reshape x1, local copies, waits for them, and re-layouts, shards(): return jnp.transpose(summed, (1, 0, 2)).reshape(1, rows, 2, width)  2.24 us

profile of v2, /device:TPU:31, one launch (start us, length us, event | category | flops | bytes accessed | tf_op | source)
XLA Modules:
  0.0 82.0 jit_solution(561177304574894775)
XLA Ops:
  0.0 79.7 %shard_map.46 = f32[2,64,1024]{2,1,0:T(8,128)} custom-call(bf16[2,1024,256]{2,1,0:T(8,128)(2,1)} %bitcast.9, bf16[2,1024,1024]{2,1,0:T(8,128)(2,1)} %bitcast.7, f32[1,1024]{1,0:T(1,128)} %bitcast.11, bf16[2,8,2,64,256]{4,3,2,1,0:T(8,128)(2,1)} %bitcast.10), custom_call_target="tpu_custom_call" | custom-call | tf_op jit(solution)/shard_map/pallas_call | solution.py:345
  79.7 2.2 %copy.5 = f32[1,64,2,1024]{3,2,1,0:T(2,128)} copy(f32[1,64,2,1024]{3,1,2,0:T(8,128)} %bitcast.8) | data formatting | bytes 1048576 | tf_op jit(solution)/shard_map/reshape | solution.py:383

commit v3 on v2

--- a/solution.py
+++ b/solution.py
@@ -14,12 +14,13 @@
 CHUNKS = 16
 PIECES = 2
 TILE = 256
-ORDERS = ((1, 2, 4), (2, 4, 1), (4, 1, 2))
-TILE_ORDER = (0, 3, 6, 1, 4, 7, 2, 5)
+VMEM_LIMIT = 55_000_000
+ORDERS = ((1, 4, 2), (2, 4, 1), (4, 1, 2), (1, 4, 2), (2, 4, 1), (4, 2, 1), (1, 2, 4), (2, 1, 4))
+TILE_ORDER = (0, 1, 2, 3, 4, 5, 6, 7)
 
 
 def order_of(tile):
-    return ORDERS[tile // 3]
+    return ORDERS[tile]
 
 
 def chip_at(z, y, relative):
@@ -111,53 +112,6 @@
                     halfway, count, deep
                 )
 
-    @pl.when(level == 0)
-    def _():
-        src_copy.wait()
-        turn_source(0)
-
-    inner = (level > 0) & (level < levels - 1)
-
-    @pl.when(inner)
-    def _():
-        pl.semaphore_wait(barrier, len(sides) + 2)
-
-    @pl.when(jnp.logical_not(inner))
-    def _():
-        pl.semaphore_wait(barrier, len(sides) + 1)
-
-    def u_swap(r):
-        return pltpu.make_async_remote_copy(
-            u_hbm.at[:, block_at(r), 1 - core], u_ref.at[1, :, r], usend_sem.at[r], urecv_sem.at[r],
-            device_id=partner, device_id_type=MESH,
-        )
-
-    for r in range(kept):
-        u_swap(r).start()
-
-    t_copy.wait()
-    for m in range(tiles):
-        w_copies[m].wait()
-
-        @pl.when(level > 0)
-        def _():
-            for k in range(PIECES):
-                for plane in range(2):
-                    block = w_ref[plane, pl.ds(m * TILE, TILE), pl.ds(k * deep, deep)]
-                    wt_ref[k, pl.ds(plane * deep, deep), pl.ds(m * TILE, TILE)] = block.T
-
-    def onward(c, k):
-        return pltpu.make_async_remote_copy(
-            q_ref.at[0, c, k], p_ref.at[c, k], psend_sem.at[c, k], precv_sem.at[c, k],
-            device_id=after, device_id_type=MESH,
-        )
-
-    def across(c):
-        return pltpu.make_async_remote_copy(
-            q_ref.at[0, c], q_ref.at[1, c], qsend_sem.at[c], qrecv_sem.at[c],
-            device_id=partner, device_id_type=MESH,
-        )
-
     def chunk_lhs(c, k):
         real = p_ref[c, k, pl.ds(0, count), :]
         imag = p_ref[c, k, pl.ds(count, count), :]
@@ -166,7 +120,7 @@
     def scaled(total, m):
         return (total * t_ref[:, pl.ds(m * deep, deep)]).astype(BF16)
 
-    def open_chunks(b):
+    def open_chunks(b, arrive=lambda m: None):
         sides = [[chunk_lhs(2 * b + i, k) for k in range(PIECES)] for i in range(2)]
         plain, turned = (
             jnp.concatenate(
@@ -175,15 +129,73 @@
             for which in range(2)
         )
         for m in range(PIECES):
+            arrive(m)
             cols = pl.ds(m * deep, deep)
             total = scaled(dot_nt(plain, w_ref[0, cols, :]) + dot_nt(turned, w_ref[1, cols, :]), m)
             for i in range(2):
                 q_ref[0, 2 * b + i, m] = total[i * 2 * count:(i + 1) * 2 * count]
-                onward(2 * b + i, m).start()
+
+    @pl.when(level == 0)
+    def _():
+        src_copy.wait()
+        turn_source(0)
+        t_copy.wait()
+
+        def arrive(m):
+            for i in range(tiles // PIECES):
+                w_copies[m * (tiles // PIECES) + i].wait()
+
+        open_chunks(0, arrive)
+
+    inner = (level > 0) & (level < levels - 1)
+
+    @pl.when(inner)
+    def _():
+        pl.semaphore_wait(barrier, len(sides) + 2)
+
+    @pl.when(jnp.logical_not(inner))
+    def _():
+        pl.semaphore_wait(barrier, len(sides) + 1)
+
+    def u_swap(r):
+        return pltpu.make_async_remote_copy(
+            u_hbm.at[:, block_at(r), 1 - core], u_ref.at[1, :, r], usend_sem.at[r], urecv_sem.at[r],
+            device_id=partner, device_id_type=MESH,
+        )
+
+    for r in range(kept):
+        u_swap(r).start()
+
+    @pl.when(level > 0)
+    def _():
+        t_copy.wait()
+        for m in range(tiles):
+            w_copies[m].wait()
+            for k in range(PIECES):
+                for plane in range(2):
+                    block = w_ref[plane, pl.ds(m * TILE, TILE), pl.ds(k * deep, deep)]
+                    wt_ref[k, pl.ds(plane * deep, deep), pl.ds(m * TILE, TILE)] = block.T
+
+    def onward(c, k):
+        return pltpu.make_async_remote_copy(
+            q_ref.at[0, c, k], p_ref.at[c, k], psend_sem.at[c, k], precv_sem.at[c, k],
+            device_id=after, device_id_type=MESH,
+        )
+
+    def across(c):
+        return pltpu.make_async_remote_copy(
+            q_ref.at[0, c], q_ref.at[1, c], qsend_sem.at[c], qrecv_sem.at[c],
+            device_id=partner, device_id_type=MESH,
+        )
+
+    def leave_chunks(b):
+        for i in range(2):
+            for k in range(PIECES):
+                onward(2 * b + i, k).start()
         for i in range(2):
             across(2 * b + i).start()
 
-    def advance(c):
+    def advance(c, last):
         totals = [None] * PIECES
         for k in range(PIECES):
             onward(c, k).wait_recv()
@@ -193,9 +205,7 @@
                 totals[m] = part if k == 0 else totals[m] + part
                 if k == PIECES - 1:
                     q_ref[0, c, m] = scaled(totals[m], m)
-
-                    @pl.when(level < levels - 1)
-                    def _():
+                    if not last:
                         onward(c, m).start()
 
         across(c).start()
@@ -230,20 +240,23 @@
     def _():
         def opening(b, carry):
             open_chunks(b)
+            leave_chunks(b)
             return carry
 
-        lax.fori_loop(0, halfway // 2, opening, 0)
+        leave_chunks(0)
+        lax.fori_loop(1, halfway // 2, opening, 0)
         turn_source(1)
         lax.fori_loop(halfway // 2, halfway, opening, 0)
         swapped()
+
         ready(0)
+        ready(1)
         for tile in range(2 * tiles):
             first_half(tile)
 
-    @pl.when(level > 0)
-    def _():
+    def run(last):
         def early(c, carry):
-            advance(c)
+            advance(c, last)
             return carry
 
         lax.fori_loop(0, halfway, early, 0)
@@ -251,13 +264,20 @@
         ready(0)
         for plane in range(2):
             def late(col, carry):
-                advance(halfway + plane * tiles + col)
+                advance(halfway + plane * tiles + col, last)
                 acc_ref[plane * tiles + col] = product(0, plane, col)
                 return carry
 
             lax.fori_loop(0, tiles, late, 0)
-
-    ready(1)
+        ready(1)
+
+    @pl.when(inner)
+    def _():
+        run(False)
+
+    @pl.when(level == levels - 1)
+    def _():
+        run(True)
 
     landing = (r1_ref, r2_ref, r3_ref)
 
@@ -308,7 +328,10 @@
         piece(tile, 0, a).wait_recv()
         total = own(tile, 0) + r1_ref[tile, 0].astype(F32)
         total = total + r2_ref[tile, 0].astype(F32) + r3_ref[tile, 0].astype(F32)
-        out_ref[tile // tiles, :, pl.ds((tile % tiles) * TILE, TILE)] = total * scale
+        total = total * scale
+        for i in range(TILE // 128):
+            at = (tile % tiles * (TILE // 128) + i) * 2 + tile // tiles
+            out_ref[pl.ds(at, rows, stride=width // 64), :] = total[:, i * 128:(i + 1) * 128]
 
     for r in range(kept):
         u_swap(r).wait_send()
@@ -344,7 +367,7 @@
     dma = pltpu.SemaphoreType.DMA
     summed = pl.pallas_call(
         functools.partial(kernel, levels, scale),
-        out_shape=jax.ShapeDtypeStruct((2, rows, width), F32),
+        out_shape=jax.ShapeDtypeStruct((rows * 2 * width // 128, 128), F32),
         in_specs=[pl.BlockSpec(memory_space=pl.ANY)] * 4,
         out_specs=pl.BlockSpec(memory_space=pltpu.VMEM),
         scratch_shapes=[
@@ -372,7 +395,7 @@
             dma((2 * tiles, 7)),
         ],
         compiler_params=pltpu.CompilerParams(
-            collective_id=0, has_side_effects=True, vmem_limit_bytes=60 * 1024 * 1024
+            collective_id=0, has_side_effects=True, vmem_limit_bytes=VMEM_LIMIT
         ),
     )(
         source.reshape(2, width, shots),
@@ -380,7 +403,8 @@
         transmission.reshape(1, width),
         upgoing.reshape(2, kept, 2, rows, shots),
     )
-    return jnp.transpose(summed, (1, 0, 2)).reshape(1, rows, 2, width)
+    summed = summed.reshape(rows, width // 128, 2, 128)
+    return jnp.transpose(summed, (0, 2, 1, 3)).reshape(1, rows, 2, width)
 
 
 def solution(mesh):

time: 82.1 us -> 79.1 us (0.963)
  Pallas kernels: 79.7 us -> 77.4 us
    pallas_call x1, Pallas kernels: 79.7 us -> 77.4 us  [shards(): pl.pallas_call(functools.partial(kernel, levels, scale), out_shape=jax.Sh...]
    reshape x1 -> x0, local copies, waits for them, and re-layouts: 2.24 us -> none  [shards(): return jnp.transpose(summed, (1, 0, 2)).reshape(1, rows, 2, width)]
    unnamed x0 -> x3, local copies, waits for them, and re-layouts: none -> 1.48 us
where the time goes in v3:
time: 79.1 us; the launch traced here: 78.9 us
  Pallas kernels  77.4 us (98%)
  local copies, waits for them, and re-layouts  1.48 us (2%)
    pallas_call x1, Pallas kernels, shards(): pl.pallas_call(functools.partial(kernel, levels, scale), out_shape=jax.Sh...  77.4 us

profile of v3, /device:TPU:31, one launch (start us, length us, event | category | flops | bytes accessed | tf_op | source)
XLA Modules:
  0.0 78.9 jit_solution(318001761662738243)
XLA Ops:
  0.0 0.0 copy-start
  0.0 0.7 copy-done
  0.7 77.4 %shard_map.46 = f32[1024,128]{1,0:T(8,128)S(1)} custom-call(bf16[2,1024,256]{2,1,0:T(8,128)(2,1)} %bitcast.12, bf16[2,1024,1024]{2,1,0:T(8,128)(2,1)} %bitcast.11, f32[1,1024]{1,0:T(1,128)S(1)} %bitcast.10, bf16[2,8,2,64,256]{4,3,2,1,0:T(8,128)(2,1)} %bitcast.13), custom_call_target="tpu_custom_call" | custom-call | tf_op jit(solution)/shard_map/pallas_call | solution.py:368
  78.1 0.8 %copy.7 = f32[1,64,2,1024]{3,2,1,0:T(2,128)} copy(f32[1,64,2,1024]{3,2,1,0:T(2,128)S(1)} %bitcast.9) | data formatting | bytes 1048576
Async XLA Ops:
  0.0 0.7 copy-start

commit v4 on v3

--- a/solution.py
+++ b/solution.py
@@ -69,8 +69,13 @@
     rows = u_ref.shape[3]
     tiles = width // TILE
 
-    src_copy = pltpu.make_async_copy(src_hbm, src_ref, load_sem.at[0])
-    t_copy = pltpu.make_async_copy(t_hbm, t_ref, load_sem.at[1])
+    src_copies = [
+        pltpu.make_async_copy(
+            src_hbm.at[:, :, pl.ds(part * half, half)], src_ref.at[part], load_sem.at[2 + tiles + part]
+        )
+        for part in range(2)
+    ]
+    t_copy = pltpu.make_async_copy(t_hbm, t_ref, load_sem.at[0])
     w_copies = [
         pltpu.make_async_copy(
             w_hbm.at[:, pl.ds(m * TILE, TILE), :], w_ref.at[:, pl.ds(m * TILE, TILE), :], load_sem.at[2 + m]
@@ -83,13 +88,11 @@
 
     @pl.when(level == 0)
     def _():
-        src_copy.start()
+        src_copies[0].start()
 
     for copy in w_copies:
         copy.start()
     t_copy.start()
-    for copy in u_copies:
-        copy.start()
 
     barrier = pltpu.get_barrier_semaphore()
     sides = [partner] + [(level, freq_at(bit)) for bit in (1, 2, 4)]
@@ -107,7 +110,7 @@
     def turn_source(part):
         for k in range(PIECES):
             for plane in range(2):
-                block = src_ref[plane, pl.ds(k * deep, deep), pl.ds(part * half, half)].T
+                block = src_ref[part, plane, pl.ds(k * deep, deep), :].T
                 p_ref[pl.ds(part * halfway, halfway), k, pl.ds(plane * count, count), :] = block.reshape(
                     halfway, count, deep
                 )
@@ -120,32 +123,33 @@
     def scaled(total, m):
         return (total * t_ref[:, pl.ds(m * deep, deep)]).astype(BF16)
 
-    def open_chunks(b, arrive=lambda m: None):
+    def open_piece(b, m, both):
+        cols = pl.ds(m * deep, deep)
+        plain, turned = both
+        total = scaled(dot_nt(plain, w_ref[0, cols, :]) + dot_nt(turned, w_ref[1, cols, :]), m)
+        for i in range(2):
+            q_ref[0, 2 * b + i, m] = total[i * 2 * count:(i + 1) * 2 * count]
+
+    def open_lhs(b):
         sides = [[chunk_lhs(2 * b + i, k) for k in range(PIECES)] for i in range(2)]
-        plain, turned = (
+        return [
             jnp.concatenate(
                 [jnp.concatenate([sides[i][k][which] for i in range(2)], axis=0) for k in range(PIECES)], axis=1
             )
             for which in range(2)
-        )
-        for m in range(PIECES):
-            arrive(m)
-            cols = pl.ds(m * deep, deep)
-            total = scaled(dot_nt(plain, w_ref[0, cols, :]) + dot_nt(turned, w_ref[1, cols, :]), m)
-            for i in range(2):
-                q_ref[0, 2 * b + i, m] = total[i * 2 * count:(i + 1) * 2 * count]
+        ]
+
+    def arrive(m):
+        for i in range(tiles // PIECES):
+            w_copies[m * (tiles // PIECES) + i].wait()
 
     @pl.when(level == 0)
     def _():
-        src_copy.wait()
+        src_copies[0].wait()
         turn_source(0)
         t_copy.wait()
-
-        def arrive(m):
-            for i in range(tiles // PIECES):
-                w_copies[m * (tiles // PIECES) + i].wait()
-
-        open_chunks(0, arrive)
+        arrive(0)
+        open_piece(0, 0, open_lhs(0))
 
     inner = (level > 0) & (level < levels - 1)
 
@@ -156,6 +160,38 @@
     @pl.when(jnp.logical_not(inner))
     def _():
         pl.semaphore_wait(barrier, len(sides) + 1)
+
+    def onward(c, k):
+        return pltpu.make_async_remote_copy(
+            q_ref.at[0, c, k], p_ref.at[c, k], psend_sem.at[c, k], precv_sem.at[c, k],
+            device_id=after, device_id_type=MESH,
+        )
+
+    def across(c):
+        return pltpu.make_async_remote_copy(
+            q_ref.at[0, c], q_ref.at[1, c], qsend_sem.at[c], qrecv_sem.at[c],
+            device_id=partner, device_id_type=MESH,
+        )
+
+    def leave_chunks(b):
+        for i in range(2):
+            for k in range(PIECES):
+                onward(2 * b + i, k).start()
+        for i in range(2):
+            across(2 * b + i).start()
+
+    @pl.when(level == 0)
+    def _():
+        onward(0, 0).start()
+        for m in range(1, PIECES):
+            arrive(m)
+            open_piece(0, m, open_lhs(0))
+            onward(0, m).start()
+        for m in range(PIECES):
+            onward(1, m).start()
+        for i in range(2):
+            across(i).start()
+        src_copies[1].start()
 
     def u_swap(r):
         return pltpu.make_async_remote_copy(
@@ -165,6 +201,7 @@
 
     for r in range(kept):
         u_swap(r).start()
+        u_copies[r].start()
 
     @pl.when(level > 0)
     def _():
@@ -175,25 +212,6 @@
                 for plane in range(2):
                     block = w_ref[plane, pl.ds(m * TILE, TILE), pl.ds(k * deep, deep)]
                     wt_ref[k, pl.ds(plane * deep, deep), pl.ds(m * TILE, TILE)] = block.T
-
-    def onward(c, k):
-        return pltpu.make_async_remote_copy(
-            q_ref.at[0, c, k], p_ref.at[c, k], psend_sem.at[c, k], precv_sem.at[c, k],
-            device_id=after, device_id_type=MESH,
-        )
-
-    def across(c):
-        return pltpu.make_async_remote_copy(
-            q_ref.at[0, c], q_ref.at[1, c], qsend_sem.at[c], qrecv_sem.at[c],
-            device_id=partner, device_id_type=MESH,
-        )
-
-    def leave_chunks(b):
-        for i in range(2):
-            for k in range(PIECES):
-                onward(2 * b + i, k).start()
-        for i in range(2):
-            across(2 * b + i).start()
 
     def advance(c, last):
         totals = [None] * PIECES
@@ -210,11 +228,11 @@
 
         across(c).start()
 
-    def product(part, plane, col):
+    def product(part, plane, col, slots=(0, 1)):
         first = part * halfway
         k, cols = col * TILE // deep, pl.ds(pl.multiple_of(col * TILE % deep, TILE), TILE)
         lhs, rhs = [], []
-        for slot in range(2):
+        for slot in slots:
             real = q_ref[slot, pl.ds(first, halfway), k, pl.ds(0, count), cols].reshape(half, TILE)
             imag = q_ref[slot, pl.ds(first, halfway), k, pl.ds(count, count), cols].reshape(half, TILE)
             u_real, u_imag = (
@@ -227,6 +245,10 @@
     def first_half(tile):
         acc_ref[tile] = product(0, tile // tiles, tile % tiles)
 
+    def own_half():
+        for tile in range(2 * tiles):
+            acc_ref[tile] += product(1, tile // tiles, tile % tiles, (0,))
+
     def ready(part):
         for c in range(part * halfway, (part + 1) * halfway):
             across(c).wait_recv()
@@ -239,12 +261,14 @@
     @pl.when(level == 0)
     def _():
         def opening(b, carry):
-            open_chunks(b)
+            both = open_lhs(b)
+            for m in range(PIECES):
+                open_piece(b, m, both)
             leave_chunks(b)
             return carry
 
-        leave_chunks(0)
         lax.fori_loop(1, halfway // 2, opening, 0)
+        src_copies[1].wait()
         turn_source(1)
         lax.fori_loop(halfway // 2, halfway, opening, 0)
         swapped()
@@ -253,6 +277,7 @@
         ready(1)
         for tile in range(2 * tiles):
             first_half(tile)
+        own_half()
 
     def run(last):
         def early(c, carry):
@@ -269,6 +294,7 @@
                 return carry
 
             lax.fori_loop(0, tiles, late, 0)
+        own_half()
         ready(1)
 
     @pl.when(inner)
@@ -296,7 +322,7 @@
 
     for tile in TILE_ORDER:
         a, b, c = order_of(tile)
-        acc_ref[tile] += product(1, tile // tiles, tile % tiles)
+        acc_ref[tile] += product(1, tile // tiles, tile % tiles, (1,))
         for r in (a + b + c, a + b, a + c):
             s_ref[tile, r] = own(tile, r).astype(BF16)
             piece(tile, 0, r).start()
@@ -371,7 +397,7 @@
         in_specs=[pl.BlockSpec(memory_space=pl.ANY)] * 4,
         out_specs=pl.BlockSpec(memory_space=pltpu.VMEM),
         scratch_shapes=[
-            pltpu.VMEM((2, width, shots), BF16),
+            pltpu.VMEM((2, 2, width, shots // 2), BF16),
             pltpu.VMEM((2, width, width), BF16),
             pltpu.VMEM((PIECES, 2 * deep, width), BF16),
             pltpu.VMEM((1, width), F32),
@@ -383,7 +409,7 @@
             pltpu.VMEM((2 * tiles, kept, rows, TILE), BF16),
             pltpu.VMEM((2 * tiles, kept, rows, TILE), BF16),
             pltpu.VMEM((2 * tiles, kept, rows, TILE), BF16),
-            dma((2 + tiles,)),
+            dma((4 + tiles,)),
             dma((kept,)),
             dma((kept,)),
             dma((kept,)),
@@ -400,7 +426,7 @@
     )(
         source.reshape(2, width, shots),
         propagator.reshape(2, width, width),
-        transmission.reshape(1, width),
+        pltpu.with_memory_space_constraint(transmission.reshape(1, width), pltpu.HBM),
         upgoing.reshape(2, kept, 2, rows, shots),
     )
     summed = summed.reshape(rows, width // 128, 2, 128)

time: 79.1 us -> 77.3 us (0.977)
  Pallas kernels: 77.4 us -> 76 us
    pallas_call x1, Pallas kernels: 77.4 us -> 76 us  [shards(): pl.pallas_call(functools.partial(kernel, levels, scale), out_shape=jax.Sh...]
where the time goes in v4:
time: 77.3 us; the launch traced here: 76.8 us
  Pallas kernels  76 us (98%)
  local copies, waits for them, and re-layouts  0.8 us (1%)
    pallas_call x1, Pallas kernels, shards(): pl.pallas_call(functools.partial(kernel, levels, scale), out_shape=jax.Sh...  76 us

profile of v4, /device:TPU:31, one launch (start us, length us, event | category | flops | bytes accessed | tf_op | source)
XLA Modules:
  0.0 76.8 jit_solution(7719187539922346941)
XLA Ops:
  0.0 76.0 %shard_map.46 = f32[1024,128]{1,0:T(8,128)S(1)} custom-call(bf16[2,1024,256]{2,1,0:T(8,128)(2,1)} %bitcast.11, bf16[2,1024,1024]{2,1,0:T(8,128)(2,1)} %bitcast.10, f32[1,1024]{1,0:T(1,128)} %bitcast.13, bf16[2,8,2,64,256]{4,3,2,1,0:T(8,128)(2,1)} %bitcast.12), custom_call_target="tpu_custom_call" | custom-call | tf_op jit(solution)/shard_map/pallas_call | solution.py:394
  76.0 0.8 %copy.7 = f32[1,64,2,1024]{3,2,1,0:T(2,128)} copy(f32[1,64,2,1024]{3,2,1,0:T(2,128)S(1)} %bitcast.9) | data formatting | bytes 1048576

commit v5 on v4

--- a/solution.py
+++ b/solution.py
@@ -86,13 +86,14 @@
         pltpu.make_async_copy(u_hbm.at[:, block_at(r), core], u_ref.at[0, :, r], uload_sem.at[r]) for r in range(kept)
     ]
 
+    t_copy.start()
+
     @pl.when(level == 0)
     def _():
         src_copies[0].start()
 
     for copy in w_copies:
         copy.start()
-    t_copy.start()
 
     barrier = pltpu.get_barrier_semaphore()
     sides = [partner] + [(level, freq_at(bit)) for bit in (1, 2, 4)]

time: 77.3 us -> 76.9 us (level)
  no operation moved by 1% of the time
where the time goes in v5:
time: 76.9 us; the launch traced here: 76.4 us
  Pallas kernels  75.6 us (98%)
  local copies, waits for them, and re-layouts  0.8 us (1%)
    pallas_call x1, Pallas kernels, shards(): pl.pallas_call(functools.partial(kernel, levels, scale), out_shape=jax.Sh...  75.6 us

profile of v5, /device:TPU:31, one launch (start us, length us, event | category | flops | bytes accessed | tf_op | source)
XLA Modules:
  0.0 76.4 jit_solution(6141358320029911054)
XLA Ops:
  0.0 75.6 %shard_map.46 = f32[1024,128]{1,0:T(8,128)S(1)} custom-call(bf16[2,1024,256]{2,1,0:T(8,128)(2,1)} %bitcast.11, bf16[2,1024,1024]{2,1,0:T(8,128)(2,1)} %bitcast.10, f32[1,1024]{1,0:T(1,128)} %bitcast.13, bf16[2,8,2,64,256]{4,3,2,1,0:T(8,128)(2,1)} %bitcast.12), custom_call_target="tpu_custom_call" | custom-call | tf_op jit(solution)/shard_map/pallas_call | solution.py:395
  75.6 0.8 %copy.7 = f32[1,64,2,1024]{3,2,1,0:T(2,128)} copy(f32[1,64,2,1024]{3,2,1,0:T(2,128)S(1)} %bitcast.9) | data formatting | bytes 1048576
